TPU v7x, 32 devices: a whole 2x2x4 slice. The times are simulated.
32 devices in a mesh: dp: 8 (over z, x), mp: 4 (over y, core).
Axes of the slice: x: 2, y: 2, z: 4, core: 2. Of those that a mesh axis runs over, the one named last changes fastest.
Arguments:
- tokens: bfloat16 [16384, 768], P('dp'), may hold values from -6 to 6
- cotangent: bfloat16 [16384, 768], P('dp'), may hold values from -6 to 6
- qkv_weight: bfloat16 [3, 768, 768], P(None, None, 'mp'), may hold values from -0.21875 to 0.21875
- col_bias: bfloat16 [2, 768], P(None, 'mp'), may hold values from -3 to 3
- out_weight: bfloat16 [768, 768], P('mp'), may hold values from -1.75 to 1.75
- in_weight: bfloat16 [768, 3072], P(None, 'mp'), may hold values from -0.21875 to 0.21875
- in_bias: bfloat16 [3072], P('mp'), may hold values from -3 to 3
- down_weight: bfloat16 [3072, 768], P('mp'), may hold values from -0.109375 to 0.109375
- vectors: bfloat16 [6, 768], replicated, may hold values from 0.5 to 1.5
- slot_is_long: int32 [32], P('dp'), may hold values from 0 to 1
- seq_len: int32 [32, 4], P('dp'), may hold values from 1 to 128, as said below
- master: float32 [4, 8, 221472], P('mp', 'dp'), may hold values from -0.18 to 0.18
- first_moment: float32 [4, 8, 221472], P('mp', 'dp'), as said below
- second_moment: float32 [4, 8, 221472], P('mp', 'dp'), as said below
- average: float32 [4, 8, 221472], P('mp', 'dp'), may hold values from -0.18 to 0.18
Outputs:
- output: bfloat16 [16384, 768], P('dp')
- grad_input: float32 [16384, 768], P('dp')
- vector_grad: float32 [4, 8, 144], P('mp', 'dp')
- new_master: float32 [4, 8, 221472], P('mp', 'dp')
- new_first: float32 [4, 8, 221472], P('mp', 'dp')
- new_second: float32 [4, 8, 221472], P('mp', 'dp')
- new_average: float32 [4, 8, 221472], P('mp', 'dp')
Inputs may be any that keep to these rules, and one draw needn't show every extreme that they name: `seq_len`: in every slot one of the four entries equals 128. `first_moment`: entries of both signs, none near zero. `second_moment`: every entry positive.
All inputs are finite; a program needn't handle non-finite values.
Results may differ from a plain program's by a relative error of at most 0.02.
Values may be sent and summed in bfloat16 or wider, within the bound.
No kernel may reach another device: no remote copies, remote signals or barrier semaphores. Data moves between devices by JAX's collectives and lax.ppermute only.
A program may use at most 128 MiB of HBM per device.

v0:
```python
import jax
import jax.numpy as jnp
from jax import lax
from jax.experimental import pallas as pl
from jax.experimental.pallas import tpu as pltpu
from jax.sharding import PartitionSpec as P

HDIM = 64
SLOT_TOKENS = 512
SHORT_TOKENS = 128
STEP = 3
NORM_EPS = 1e-12
BF = jnp.bfloat16
F32 = jnp.float32


def slot_masks(kind, sequence_lengths):
    pos = jnp.arange(SLOT_TOKENS, dtype=jnp.int32)
    block = pos // SHORT_TOKENS
    is_long = kind == 1
    segment = jnp.where(is_long, 0, block)
    inner = jnp.where(is_long, pos, pos % SHORT_TOKENS)
    picks = block[:, None] == jnp.arange(sequence_lengths.shape[0], dtype=jnp.int32)[None, :]
    short_len = jnp.sum(jnp.where(picks, sequence_lengths[None, :], 0), axis=1)
    seg_len = jnp.where(is_long, jnp.sum(sequence_lengths), short_len)
    valid = inner < seg_len
    allowed = (segment[:, None] == segment[None, :]) & valid[None, :]
    return (allowed, valid)


def dot(a, b):
    return lax.dot_general(a, b, (((1,), (0,)), ((), ())), preferred_element_type=F32)


def dot_t(a, b):
    return lax.dot_general(a, b, (((1,), (1,)), ((), ())), preferred_element_type=F32)


def t_dot(a, b):
    return lax.dot_general(a, b, (((0,), (0,)), ((), ())), preferred_element_type=F32)


def swap(value, axis, bit):
    size = lax.axis_size(axis)
    return lax.ppermute(value, axis, [(i, i ^ bit) for i in range(size)])


def both_cores(value):
    return (value, swap(value, "mp", 1))


def norm_parts(z):
    mean = jnp.mean(z, axis=-1, keepdims=True)
    centered = z - mean
    var = jnp.mean(centered * centered, axis=-1, keepdims=True)
    rstd = lax.rsqrt(var + NORM_EPS)
    return centered * rstd, rstd


def norm_back(dy, normed, rstd, gain):
    dn = dy * gain
    back = rstd * (
        dn
        - jnp.mean(dn, axis=-1, keepdims=True)
        - normed * jnp.mean(dn * normed, axis=-1, keepdims=True)
    )
    return back, jnp.sum(dy * normed, axis=0), jnp.sum(dy, axis=0), jnp.sum(back, axis=0)


VMEM = pl.BlockSpec(memory_space=pltpu.VMEM)
SMEM = pl.BlockSpec(memory_space=pltpu.SMEM)


def struct(shape, dtype):
    return jax.ShapeDtypeStruct(shape, dtype)


def key_codes(kind, lens, axis):
    shape = (SLOT_TOKENS, 1) if axis == 0 else (1, SLOT_TOKENS)
    pos = lax.broadcasted_iota(jnp.int32, shape, axis)
    block = pos >> 7
    short = jnp.where(
        block == 0, lens[0], jnp.where(block == 1, lens[1], jnp.where(block == 2, lens[2], lens[3]))
    )
    is_long = kind == 1
    inner = jnp.where(is_long, pos, pos & (SHORT_TOKENS - 1))
    length = jnp.where(is_long, lens[0] + lens[1] + lens[2] + lens[3], short)
    return jnp.where(inner < length, jnp.where(is_long, 0, block), -1)


def query_codes(kind, axis):
    shape = (SLOT_TOKENS, 1) if axis == 0 else (1, SLOT_TOKENS)
    pos = lax.broadcasted_iota(jnp.int32, shape, axis)
    return jnp.where(kind == 1, 0, pos >> 7)


def slot_info(info_ref):
    return info_ref[0], [info_ref[1 + i] for i in range(4)]


def forward_kernel(info, x, w, bias, wo, q_out, k_out, v_out, ctx_out, lse_out, part):
    kind, lens = slot_info(info)
    wide = ctx_out.shape[1]
    scale = HDIM ** (-0.5)
    xv = x[...]
    q_out[...] = ((dot_t(xv, w[:wide]) + bias[0:1]) * scale).astype(BF)
    k_out[...] = dot_t(xv, w[wide : 2 * wide]).astype(BF)
    v_out[...] = (dot_t(xv, w[2 * wide :]) + bias[1:2]).astype(BF)
    allowed = query_codes(kind, 0) == key_codes(kind, lens, 1)
    lower = lax.broadcasted_iota(jnp.int32, (1, 128), 1) < HDIM

    @pl.loop(0, wide // 128)
    def _(pair):
        at = pl.ds(pl.multiple_of(pair * 128, 128), 128)
        q, k, v = q_out[:, at], k_out[:, at], v_out[:, at]
        results = []
        for half in (lower, ~lower):
            s = dot_t(jnp.where(half, q, jnp.zeros_like(q)), k)
            s = jnp.where(allowed, s, -1000000000.0)
            top = jnp.max(s, axis=-1, keepdims=True)
            e = jnp.exp(s - top)
            total = jnp.sum(e, axis=-1, keepdims=True)
            results.append((dot(e.astype(BF), v) / total, top + jnp.log(total)))
        (ctx0, lse0), (ctx1, lse1) = results
        ctx_out[:, at] = jnp.where(lower, ctx0, ctx1).astype(BF)
        lse_out[:, at] = jnp.where(lower, lse0, lse1)

    part[...] = dot(ctx_out[...], wo[...]).astype(BF)


def backward_kernel(
    info, dz_two, own, other, normed, rstd, gain, q_in, k_in, v_in, ctx_in, lse_in, w, wo,
    dz_out, dzb_out, dq_out, dk_out, dv_out, sums, part, dctx,
):
    kind, lens = slot_info(info)
    wide = ctx_in.shape[1]
    scale = HDIM ** (-0.5)
    dx = dz_two[...] + (own[...].astype(F32) + other[...].astype(F32))
    unit = normed[...]
    dn = dx * gain[...]
    back = rstd[...] * (
        dn
        - jnp.mean(dn, axis=-1, keepdims=True)
        - unit * jnp.mean(dn * unit, axis=-1, keepdims=True)
    )
    dz_out[...] = back
    dzb_out[...] = back.astype(BF)
    sums[0:1] = jnp.sum(dx * unit, axis=0, keepdims=True)
    sums[1:2] = jnp.sum(dx, axis=0, keepdims=True)
    sums[2:3] = jnp.sum(back, axis=0, keepdims=True)
    sums[3:] = jnp.zeros((sums.shape[0] - 3, sums.shape[1]), F32)
    dctx[...] = dot_t(dzb_out[...], wo[...]).astype(BF)
    allowed = key_codes(kind, lens, 0) == query_codes(kind, 1)
    lower = lax.broadcasted_iota(jnp.int32, (1, 128), 1) < HDIM

    @pl.loop(0, wide // 128)
    def _(pair):
        at = pl.ds(pl.multiple_of(pair * 128, 128), 128)
        q, k, v, dc = q_in[:, at], k_in[:, at], v_in[:, at], dctx[:, at]
        lse_t = jnp.transpose(lse_in[:, at])
        prod_t = jnp.transpose(dc.astype(F32) * ctx_in[:, at].astype(F32))
        results = []
        for number, half in enumerate((lower, ~lower)):
            base = number * HDIM
            s = dot_t(k, jnp.where(half, q, jnp.zeros_like(q)))
            p = jnp.where(allowed, jnp.exp(s - lse_t[base : base + 1]), 0.0)
            dp = dot_t(v, jnp.where(half, dc, jnp.zeros_like(dc)))
            row = jnp.sum(prod_t[base : base + HDIM], axis=0, keepdims=True)
            ds = (p * (dp - row)).astype(BF)
            results.append((t_dot(ds, k), dot(ds, q), dot(p.astype(BF), dc)))
        for out, a, b in zip((dq_out, dk_out, dv_out), *results):
            out[:, at] = jnp.where(lower, a, b).astype(BF)

    part[...] = (
        dot(dq_out[...], w[:wide]) * scale
        + dot(dk_out[...], w[wide : 2 * wide])
        + dot(dv_out[...], w[2 * wide :])
    ).astype(BF)


def gradient_kernel(blocks, x, dq0, dq1, dk0, dk1, dv0, dv1, own, other, columns):
    scale = HDIM ** (-0.5)
    depth = own.shape[1]
    cols = own.shape[2]
    for piece, pair in enumerate(((dq0, dq1), (dk0, dk1), (dv0, dv1))):
        g = t_dot(x[:SLOT_TOKENS], pair[0][...]) + t_dot(x[SLOT_TOKENS:], pair[1][...])
        if piece == 0:
            g = g * scale
        mine, theirs = g[:, :cols], g[:, cols:]
        wide = g.shape[0]
        row = 0
        while row < wide:
            block, inside = divmod(piece * wide + row, depth)
            take = min(wide - row, depth - inside)
            own[block, inside : inside + take] = mine[row : row + take]
            other[block, inside : inside + take] = theirs[row : row + take].astype(BF)
            row += take
        total = jnp.sum(pair[0][...].astype(F32), axis=0, keepdims=True) + jnp.sum(
            pair[1][...].astype(F32), axis=0, keepdims=True
        )
        columns[piece : piece + 1] = total * (scale if piece == 0 else 1.0)
    columns[3:] = jnp.zeros((columns.shape[0] - 3, columns.shape[1]), F32)


def call(kernel, inputs, outputs, scratch=(), flops=0, name=None):
    size = sum(a.size * a.dtype.itemsize for a in list(inputs[0:]) + list(outputs))
    return pl.pallas_call(
        kernel,
        in_specs=[SMEM if a.ndim == 1 else VMEM for a in inputs],
        out_specs=[VMEM] * len(outputs),
        out_shape=list(outputs),
        scratch_shapes=list(scratch),
        cost_estimate=pl.CostEstimate(flops=flops, bytes_accessed=size, transcendentals=0),
        name=name,
    )(*inputs)


def scatter_sum(blocks, first, order):
    ndata = blocks.shape[0]
    rank = lax.axis_index("dp")
    cur = blocks[None]
    left = list(range(ndata.bit_length() - 1))
    for bit in order(left):
        low = sum(1 for b in left if b < bit)
        rest = cur.shape[2:]
        view = cur.reshape((cur.shape[1] >> (low + 1), 2, 1 << low) + rest)
        mine = (rank >> bit) & 1
        keep = lax.dynamic_index_in_dim(view, mine, 1, keepdims=False)
        send = lax.dynamic_index_in_dim(view, 1 - mine, 1, keepdims=False)
        got = swap(send.astype(BF), "dp", 1 << bit)
        cur = (keep.astype(F32) + got.astype(F32)).reshape((1, -1) + rest)
        left.remove(bit)
    return cur[0, 0]


def upward(left):
    return list(left)


def body(
    tokens,
    cotangent,
    qkv_weight,
    col_bias,
    out_weight,
    in_weight,
    in_bias,
    down_weight,
    vectors,
    slot_is_long,
    seq_len,
    master,
    first_moment,
    second_moment,
    average,
):
    rows = tokens.shape[0]
    scale = HDIM ** (-0.5)
    ndata = lax.axis_size("dp")
    nmodel = lax.axis_size("mp")
    core = lax.axis_index("mp") & 1
    pair = lax.axis_index("mp") >> 1
    vec = vectors.astype(F32)
    per_core = rows // 2 // SLOT_TOKENS

    cols = qkv_weight.shape[2]
    wide = 2 * cols
    wqkv = both_cores(jnp.transpose(qkv_weight, (0, 2, 1)))
    w_attn = jnp.concatenate(wqkv, axis=1).reshape(3 * wide, -1)
    bias = jnp.concatenate(both_cores(col_bias), axis=1).astype(F32)
    wo = jnp.concatenate(both_cores(out_weight), axis=0)
    w1 = both_cores(in_weight)
    b1 = both_cores(in_bias)
    w2 = both_cores(down_weight)
    model = tokens.shape[1]
    slot_flops = 2 * SLOT_TOKENS * model * wide

    x_mine = lax.dynamic_slice_in_dim(tokens, core * (rows // 2), rows // 2)
    cot_mine = lax.dynamic_slice_in_dim(cotangent, core * (rows // 2), rows // 2)
    kinds = lax.dynamic_slice_in_dim(slot_is_long, core * per_core, per_core)
    lengths = lax.dynamic_slice_in_dim(seq_len, core * per_core, per_core)
    n = range(per_core)
    info = [jnp.concatenate([kinds[i : i + 1], lengths[i]]) for i in n]
    x = [x_mine[i * SLOT_TOKENS : (i + 1) * SLOT_TOKENS] for i in n]
    cot = [cot_mine[i * SLOT_TOKENS : (i + 1) * SLOT_TOKENS] for i in n]
    masks = [slot_masks(kinds[i], lengths[i]) for i in n]

    def phase_one(i):
        act = struct((SLOT_TOKENS, wide), BF)
        *kept, part = call(
            forward_kernel,
            (info[i], x[i], w_attn, bias, wo),
            (act, act, act, act, struct((SLOT_TOKENS, wide), F32), struct((SLOT_TOKENS, model), BF)),
            flops=6 * slot_flops,
            name="attn_fwd",
        )
        return kept, part

    def total(part, other):
        return part.astype(F32) + other.astype(F32)

    def phase_two(i, part, other):
        z = x[i].astype(F32) + total(part, other) + vec[4]
        normed, rstd = norm_parts(z)
        x_one = normed * vec[0] + vec[1]
        xb = x_one.astype(BF)
        hidden, slope, out = [], [], 0.0
        for g in range(2):
            pre = dot(xb, w1[g]) + b1[g].astype(F32)
            phi = 0.5 * (1.0 + lax.erf(pre * 2.0 ** (-0.5)))
            hidden.append((pre * phi).astype(BF))
            bell = jnp.exp(-0.5 * pre * pre) * 0.3989422804014327
            slope.append((phi + pre * bell).astype(BF))
            out = out + dot(hidden[g], w2[g])
        return (normed, rstd, x_one, xb, hidden, slope), out.astype(BF)

    def phase_three(i, saved, part, other):
        normed, rstd, x_one, xb, hidden, slope = saved
        z = x_one + total(part, other) + vec[5]
        n2, r2 = norm_parts(z)
        out = (n2 * vec[2] + vec[3]).astype(BF)
        dy = cot[i].astype(F32) * masks[i][1][:, None].astype(F32)
        dz, dg, dbeta, db = norm_back(dy, n2, r2, vec[2])
        dzb = dz.astype(BF)
        dpre, back = [], 0.0
        for g in range(2):
            dpre.append((dot_t(dzb, w2[g]) * slope[g].astype(F32)).astype(BF))
            back = back + dot_t(dpre[g], w1[g])
        return out, (dz, dzb, dpre, (dg, dbeta, db)), back.astype(BF)

    def phase_four(i, first, second, third, part, other):
        q, k, v, ctx, lse = first
        normed, rstd = second[:2]
        act = struct((SLOT_TOKENS, wide), BF)
        dz, dzb, dq, dk, dv, sums, back = call(
            backward_kernel,
            (info[i], third[0], part, other, normed, rstd, vec[0:1], q, k, v, ctx, lse, w_attn, wo),
            (
                struct((SLOT_TOKENS, model), F32),
                struct((SLOT_TOKENS, model), BF),
                act,
                act,
                act,
                struct((8, model), F32),
                struct((SLOT_TOKENS, model), BF),
            ),
            scratch=(pltpu.VMEM((SLOT_TOKENS, wide), BF),),
            flops=10 * slot_flops,
            name="attn_bwd",
        )
        return (dz, dzb, (dq, dk, dv), (sums[0], sums[1], sums[2])), back

    across = lambda part: swap(part, "mp", 2)
    one = [phase_one(i) for i in n]
    one_r = [across(one[i][1]) for i in n]
    two = [phase_two(i, one[i][1], one_r[i]) for i in n]
    two_r = [across(two[i][1]) for i in n]
    three = [phase_three(i, two[i][0], two[i][1], two_r[i]) for i in n]
    three_r = [across(three[i][2]) for i in n]
    four = [phase_four(i, one[i][0], two[i][0], three[i][1], three[i][2], three_r[i]) for i in n]
    four_r = [across(four[i][1]) for i in n]

    def whole(half, other):
        first = jnp.where(core == 0, half, other)
        second = jnp.where(core == 0, other, half)
        return jnp.concatenate([first, second])

    out_half = jnp.concatenate([three[i][0] for i in n])
    output = whole(out_half, swap(out_half, "mp", 1))
    gi_half = jnp.concatenate([four[i][0][0] + total(four[i][1], four_r[i]) for i in n])
    grad_input = whole(gi_half, swap(gi_half, "mp", 1))

    def over_cores(parts):
        return parts[0] + swap(parts[1].astype(BF), "mp", 1).astype(F32)

    cat = lambda f: jnp.concatenate([f(i) for i in n])
    xb_all = cat(lambda i: two[i][0][3])
    dz2_all = cat(lambda i: three[i][1][1])
    g_down, g_in, g_inb = [], [], []
    for g in range(2):
        dpre = cat(lambda i: three[i][1][2][g])
        g_down.append(t_dot(cat(lambda i: two[i][0][4][g]), dz2_all))
        g_in.append(t_dot(xb_all, dpre))
        g_inb.append(jnp.sum(dpre.astype(F32), axis=0))
    s_down = scatter_sum(over_cores(g_down).reshape(ndata, -1, g_down[0].shape[1]), None, upward)
    s_in = scatter_sum(over_cores(g_in).reshape(ndata, -1, g_in[0].shape[1]), None, upward)

    ctx_all = cat(lambda i: one[i][0][3])
    dz1_all = cat(lambda i: four[i][0][1])
    g_full = t_dot(ctx_all, dz1_all)
    g_out = [g_full[:cols], g_full[cols:]]
    s_out = scatter_sum(over_cores(g_out).reshape(ndata, -1, model), None, upward)
    pairs = [four[i][0][2][t] for t in range(3) for i in n]
    block = (ndata, 3 * model // ndata, cols)
    g_own, g_other, g_sums = call(
        lambda *refs: gradient_kernel(ndata, *refs),
        (x_mine, *pairs),
        (struct(block, F32), struct(block, BF), struct((8, wide), F32)),
        flops=6 * slot_flops,
        name="attn_grad",
    )
    s_qkv = scatter_sum(g_own + swap(g_other, "mp", 1).astype(F32), None, upward)
    g_col = [jnp.stack([g_sums[0, c], g_sums[2, c]]) for c in (slice(0, cols), slice(cols, wide))]

    add = lambda t: sum(t[1:], t[0])
    g1, be1, bo = (add([four[i][0][3][t] for i in n]) for t in range(3))
    g2, be2, b2 = (add([three[i][1][3][t] for i in n]) for t in range(3))
    g_vec = jnp.stack([g1, be1, g2, be2, bo, b2]).reshape(nmodel, -1)
    small = []
    for g in range(2):
        owner = 2 * pair + (core if g == 0 else 1 - core)
        share = lax.dynamic_index_in_dim(g_vec, owner, 0, keepdims=False)
        small.append(
            jnp.concatenate([g_col[g].reshape(ndata, -1), g_inb[g].reshape(ndata, -1), share.reshape(ndata, -1)], axis=1)
        )
    s_small = scatter_sum(over_cores(small), None, upward)
    n_vec = g_vec.shape[1] // ndata

    grad = jnp.concatenate([s_qkv.reshape(-1), s_out.reshape(-1), s_in.reshape(-1), s_down.reshape(-1), s_small])
    grad = (grad / ndata).reshape(master.shape)
    vector_grad = (s_small[-n_vec:] / ndata).reshape(1, 1, -1)
    new_first = 0.5 * first_moment + 0.5 * grad
    new_second = 0.5 * second_moment + 0.5 * grad * grad
    corr = 1.0 - 0.5**STEP
    new_master = master - 0.02 * (
        new_first / corr / (jnp.sqrt(new_second / corr) + 1e-08) + 0.01 * master
    )
    new_average = 0.75 * average + 0.25 * new_master
    return (output, grad_input, vector_grad, new_master, new_first, new_second, new_average)


def solution(mesh):
    rows = P("dp", None)
    opt = P("mp", "dp", None)
    return jax.shard_map(
        body,
        mesh=mesh,
        in_specs=(
            rows,
            rows,
            P(None, None, "mp"),
            P(None, "mp"),
            P("mp", None),
            P(None, "mp"),
            P("mp"),
            P("mp", None),
            P(),
            P("dp"),
            rows,
            opt,
            opt,
            opt,
            opt,
        ),
        out_specs=(rows, rows, opt, opt, opt, opt, opt),
        check_vma=False,
    )
```

profile of v0, /device:TPU:0, one launch (start us, length us, event | category | flops | bytes accessed | tf_op | source)
XLA Modules:
  0.0 306.7 jit_solution(16697292390494320303)
XLA Ops:
  4.8 2.7 constant_dynamic-slice_fusion
  12.2 8.0 %attn_fwd.3 = (bf16[512,384]{1,0:T(8,128)(2,1)}, bf16[512,384]{1,0:T(8,128)(2,1)}, bf16[512,384]{1,0:T(8,128)(2,1)}, bf16[512,384]{1,0:T(8,128)(2,1)}, f32[512,384]{1,0:T(8,128)}, /*index=5*/bf16[512,768]{1,0:T(8,128)(2,1)}) custom-call(s32[5]{0:T(128)} %pad_add_fusion.1.info, bf16[512,768]{1,0:T(8,128)(2,1)} %get-tuple-element.135.x, ...), custom_call_target="tpu_custom_call" | custom-call | flops 1811939328 | bytes 6294548 | tf_op jit(solution)/shard_map/attn_fwd/pallas_call | solution.py:207
  20.2 2.6 collective-permute-start.8
  22.8 8.3 %attn_fwd.2 = (bf16[512,384]{1,0:T(8,128)(2,1)}, bf16[512,384]{1,0:T(8,128)(2,1)}, bf16[512,384]{1,0:T(8,128)(2,1)}, bf16[512,384]{1,0:T(8,128)(2,1)}, f32[512,384]{1,0:T(8,128)}, /*index=5*/bf16[512,768]{1,0:T(8,128)(2,1)}) custom-call(s32[5]{0:T(128)} %pad_add_fusion.info, bf16[512,768]{1,0:T(8,128)(2,1)} %get-tuple-element.136.x, ...), custom_call_target="tpu_custom_call" | custom-call | flops 1811939328 | bytes 6294548 | tf_op jit(solution)/shard_map/attn_fwd/pallas_call | solution.py:207
  32.4 9.0 %collective-permute-done.8 = bf16[512,768]{1,0:T(8,128)(2,1)S(1)} collective-permute-done((bf16[512,768]{1,0:T(8,128)(2,1)}, bf16[512,768]{1,0:T(8,128)(2,1)S(1)}, u32[]{:S(2)}, u32[]{:S(2)}) %collective-permute-start.8) | collective-permute-done | bytes 786464 | tf_op jit(solution)/shard_map/ppermute | solution.py:45
  41.4 16.6 %collective-permute-done.3 = bf16[512,768]{1,0:T(8,128)(2,1)S(1)} collective-permute-done((bf16[512,768]{1,0:T(8,128)(2,1)}, bf16[512,768]{1,0:T(8,128)(2,1)S(1)}, u32[]{:S(2)}, u32[]{:S(2)}) %collective-permute-start.3) | collective-permute-done | bytes 786464 | tf_op jit(solution)/shard_map/ppermute | solution.py:45
  61.1 2.8 fusion.50
  81.4 2.8 constant_dynamic-slice_fusion.11.refs_0_
  87.3 4.1 %collective-permute-done.7 = bf16[512,768]{1,0:T(8,128)(2,1)} collective-permute-done((bf16[512,768]{1,0:T(8,128)(2,1)}, bf16[512,768]{1,0:T(8,128)(2,1)}, u32[]{:S(2)}, u32[]{:S(2)}) %collective-permute-start.7) | collective-permute-done | bytes 786464 | tf_op jit(solution)/shard_map/ppermute | solution.py:45
  91.4 15.7 %collective-permute-done.9 = bf16[512,768]{1,0:T(8,128)(2,1)} collective-permute-done((bf16[512,768]{1,0:T(8,128)(2,1)}, bf16[512,768]{1,0:T(8,128)(2,1)}, u32[]{:S(2)}, u32[]{:S(2)}) %collective-permute-start.9) | collective-permute-done | bytes 786464 | tf_op jit(solution)/shard_map/ppermute | solution.py:45
  107.1 2.8 fusion.89
  133.4 2.5 fusion.47
  137.8 4.3 %fusion.44 = bf16[768,768]{1,0:T(8,128)(2,1)} fusion(bf16[512,768]{1,0:T(8,128)(2,1)} %copy-done.54, bf16[512,768]{1,0:T(8,128)(2,1)} %copy-done.53, bf16[512,768]{1,0:T(8,128)(2,1)} %copy-done.38, bf16[512,768]{1,0:T(8,128)(2,1)} %copy-done.36), kind=kOutput, calls=%fused_computation.100 | convolution fusion | flops 1214840832 | bytes 4325376 | tf_op jit(solution)/shard_map/dot_general | solution.py:40
  143.9 5.3 %collective-permute-done.13.other = bf16[512,768]{1,0:T(8,128)(2,1)} collective-permute-done((bf16[512,768]{1,0:T(8,128)(2,1)}, bf16[512,768]{1,0:T(8,128)(2,1)}, u32[]{:S(2)}, u32[]{:S(2)}) %collective-permute-start.13) | collective-permute-done | bytes 786464 | tf_op jit(solution)/shard_map/ppermute | solution.py:45
  149.2 13.8 %attn_bwd.3 = (f32[512,768]{1,0:T(8,128)}, bf16[512,768]{1,0:T(8,128)(2,1)}, bf16[512,384]{1,0:T(8,128)(2,1)}, bf16[512,384]{1,0:T(8,128)(2,1)}, bf16[512,384]{1...) custom-call(s32[5]{0:T(128)} %pad_add_fusion.1.info, f32[512,768]{1,0:T(8,128)} %copy-done.11, ...), custom_call_target="tpu_custom_call" | custom-call | flops 3019898880 | bytes 13792276 | tf_op jit(solution)/shard_map/attn_bwd/pallas_call | solution.py:207
  164.1 13.6 %attn_bwd.2 = (f32[512,768]{1,0:T(8,128)}, bf16[512,768]{1,0:T(8,128)(2,1)}, bf16[512,384]{1,0:T(8,128)(2,1)}, bf16[512,384]{1,0:T(8,128)(2,1)}, bf16[512,384]{1...) custom-call(s32[5]{0:T(128)} %pad_add_fusion.info, f32[512,768]{1,0:T(8,128)} %copy-done.10, ...), custom_call_target="tpu_custom_call" | custom-call | flops 3019898880 | bytes 13792276 | tf_op jit(solution)/shard_map/attn_bwd/pallas_call | solution.py:207
  177.7 6.8 %attn_grad.1 = (f32[8,288,192]{2,1,0:T(8,128)}, bf16[8,288,192]{2,1,0:T(8,128)(2,1)}, f32[8,384]{1,0:T(8,128)}) custom-call(bf16[1024,768]{1,0:T(8,128)(2,1)} %constant_dynamic-slice_fusion.11.refs_0_, bf16[512,384]{1,0:T(8,128)(2,1)} %get-tuple-element.52.refs_1_, bf16[512,384]{1,0:T(8,128)(2,1)} %get-tuple-element.53.refs_2_, ...), custom_call_target="tpu_custom_call" | custom-call | flops 1811939328 | bytes 6598656 | tf_op jit(solution)/shard_map/attn_grad/pallas_call | solution.py:207
  188.5 3.4 %fusion.20 = f32[384,768]{1,0:T(8,128)} fusion(bf16[512,768]{1,0:T(8,128)(2,1)} %get-tuple-element.64, bf16[512,768]{1,0:T(8,128)(2,1)} %get-tuple-element.63, bf16[512,384]{1,0:T(8,128)(2,1)} %get-tuple-element.48.ctx_in, bf16[512,384]{1,0:T(8,128)(2,1)} %get-tuple-element.41.ctx_in), kind=kOutput, calls=%fused_computation.34 | convolution fusion | flops 608698368 | bytes 3538944 | tf_op jit(solution)/shard_map/dot_general | solution.py:40
  194.9 2.1 collective-permute-done.17
  204.5 2.9 convert_add_fusion.1
  208.7 2.7 convert_add_fusion
  211.4 2.3 collective-permute-done.25
  216.0 2.2 collective-permute-done.26
  218.3 2.3 collective-permute-start.27
  223.2 2.3 collective-permute-start.19
  244.2 10.6 %collective-permute-done.33 = bf16[4,1,96,768]{3,2,0,1:T(8,128)(2,1)S(1)} collective-permute-done((bf16[4,1,96,768]{3,2,0,1:T(8,128)(2,1)S(1)}, bf16[4,1,96,768]{3,2,0,1:T(8,128)(2,1)S(1)}, u32[]{:S(2)}, u32[]{:S(2)}) %collective-permute-start.33) | collective-permute-done | bytes 589856 | tf_op jit(solution)/shard_map/ppermute | solution.py:45
  257.3 8.8 %collective-permute-done.34 = bf16[2,1,96,768]{3,2,1,0:T(8,128)(2,1)S(1)} collective-permute-done((bf16[2,1,96,768]{3,2,1,0:T(8,128)(2,1)S(1)}, bf16[2,1,96,768]{3,2,1,0:T(8,128)(2,1)S(1)}, u32[]{:S(2)}, u32[]{:S(2)}) %collective-permute-start.34) | collective-permute-done | bytes 294944 | tf_op jit(solution)/shard_map/ppermute | solution.py:45
  268.1 8.2 %collective-permute-done.22 = bf16[2,1,288,192]{3,2,1,0:T(8,128)(2,1)S(1)} collective-permute-done((bf16[2,1,288,192]{3,2,1,0:T(8,128)(2,1)S(1)}, bf16[2,1,288,192]{3,2,1,0:T(8,128)(2,1)S(1)}, u32[]{:S(2)}, u32[]{:S(2)}) %collective-permute-start.22) | collective-permute-done | bytes 221216 | tf_op jit(solution)/shard_map/ppermute | solution.py:45
  282.2 3.1 collective-permute-done.23
  291.2 9.2 %multiply_add_fusion.2 = (f32[1,1,221472]{2,1,0:T(1,128)}, f32[1,1,221472]{2,1,0:T(1,128)}, f32[1,1,221472]{2,1,0:T(1,128)}, f32[1,1,221472]{2,1,0:T(1,128)}) fusion(f32[1,1,221472]{2,1,0:T(1,128)S(1)} %copy-done.23, f32[1,1,221472]{2,1,0:T(1,128)S(1)} %copy-done.24, f32[1,1,221472]{2,1,0:T(1,128)S(1)} %get-tuple-element.115, f32[1,1,221472]{2,1,0:T(1,128)} %param.27, ...), kind=kLoop, calls=%fused_computation.119 | loop fusion | flops 3986496 | bytes 7972992 | tf_op jit(solution)/shard_map/add | solution.py:428
  301.0 2.3 broadcast_select_fusion.1
  303.3 3.1 %pad_maximum_fusion = f32[2048,768]{1,0:T(8,128)} fusion(f32[1024,768]{1,0:T(8,128)S(1)} %get-tuple-element.130, f32[1024,768]{1,0:T(8,128)S(1)} %get-tuple-element.129), kind=kLoop, calls=%fused_computation | loop fusion | flops 1572864 | bytes 12582912 | tf_op jit(solution)/shard_map/concatenate | solution.py:366
  (318 shorter events, 116.2 us)
Async XLA Ops:
  0.6 9.5 %collective-permute-start.1 = (bf16[2,192]{1,0:T(2,128)(2,1)}, bf16[2,192]{1,0:T(2,128)(2,1)S(1)}, u32[]{:S(2)}, u32[]{:S(2)}) collective-permute-start(bf16[2,192]{1,0:T(2,128)(2,1)} %param.18), channel_id=1, source_target_pairs={{0,1},{1,0},{2,3},{3,2},{4,5},{5,4},{6,7},{7,6},{8,9},{9,8},{10,11... | collective-permute-start | bytes 2312 | tf_op jit(solution)/shard_map/ppermute | solution.py:45
  1.2 9.6 %collective-permute-start.2 = (bf16[192,768]{1,0:T(8,128)(2,1)}, bf16[192,768]{1,0:T(8,128)(2,1)S(1)}, u32[]{:S(2)}, u32[]{:S(2)}) collective-permute-start(bf16[192,768]{1,0:T(8,128)(2,1)} %param.19), channel_id=1, source_target_pairs={{0,1},{1,0},{2,3},{3,2},{4,5},{5,4},{6,7},{7,6},{8,9},{9,8},{10,11... | collective-permute-start | bytes 884744 | tf_op jit(solution)/shard_map/ppermute | solution.py:45
  1.3 9.6 %collective-permute-start = (bf16[3,192,768]{2,1,0:T(8,128)(2,1)}, bf16[3,192,768]{2,1,0:T(8,128)(2,1)S(1)}, u32[]{:S(2)}, u32[]{:S(2)}) collective-permute-start(bf16[3,192,768]{2,1,0:T(8,128)(2,1)} %bitcast.142), channel_id=1, source_target_pairs={{0,1},{1,0},{2,3},{3,2},{4,5},{5,4},{6,7},{7,6},{8,9},{9,8},{10,11... | collective-permute-start | bytes 2654216 | tf_op jit(solution)/shard_map/ppermute | solution.py:45
  20.2 21.2 %collective-permute-start.8 = (bf16[512,768]{1,0:T(8,128)(2,1)}, bf16[512,768]{1,0:T(8,128)(2,1)S(1)}, u32[]{:S(2)}, u32[]{:S(2)}) collective-permute-start(bf16[512,768]{1,0:T(8,128)(2,1)} %get-tuple-element.37), channel_id=1, source_target_pairs={{0,2},{1,3},{2,0},{3,1},{4,6},{5,7},{6,4},{7,5},{8,10},{9,11},{10,... | collective-permute-start | bytes 2359304 | tf_op jit(solution)/shard_map/ppermute | solution.py:45
  31.2 26.9 %collective-permute-start.3 = (bf16[512,768]{1,0:T(8,128)(2,1)}, bf16[512,768]{1,0:T(8,128)(2,1)S(1)}, u32[]{:S(2)}, u32[]{:S(2)}) collective-permute-start(bf16[512,768]{1,0:T(8,128)(2,1)} %get-tuple-element.36), channel_id=1, source_target_pairs={{0,2},{1,3},{2,0},{3,1},{4,6},{5,7},{6,4},{7,5},{8,10},{9,11},{10,... | collective-permute-start | bytes 2359304 | tf_op jit(solution)/shard_map/ppermute | solution.py:45
  31.4 35.5 %collective-permute-start.4 = (bf16[768,768]{1,0:T(8,128)(2,1)}, bf16[768,768]{1,0:T(8,128)(2,1)S(1)}, u32[]{:S(2)}, u32[]{:S(2)}) collective-permute-start(bf16[768,768]{1,0:T(8,128)(2,1)} %param.20), channel_id=1, source_target_pairs={{0,1},{1,0},{2,3},{3,2},{4,5},{5,4},{6,7},{7,6},{8,9},{9,8},{10,11... | collective-permute-start | bytes 3538952 | tf_op jit(solution)/shard_map/ppermute | solution.py:45
  31.7 37.2 %collective-permute-start.6 = (bf16[768,768]{1,0:T(8,128)(2,1)}, bf16[768,768]{1,0:T(8,128)(2,1)S(1)}, u32[]{:S(2)}, u32[]{:S(2)}) collective-permute-start(bf16[768,768]{1,0:T(8,128)(2,1)} %param.22), channel_id=1, source_target_pairs={{0,1},{1,0},{2,3},{3,2},{4,5},{5,4},{6,7},{7,6},{8,9},{9,8},{10,11... | collective-permute-start | bytes 3538952 | tf_op jit(solution)/shard_map/ppermute | solution.py:45
  70.6 20.7 %collective-permute-start.7 = (bf16[512,768]{1,0:T(8,128)(2,1)}, bf16[512,768]{1,0:T(8,128)(2,1)}, u32[]{:S(2)}, u32[]{:S(2)}) collective-permute-start(bf16[512,768]{1,0:T(8,128)(2,1)} %add_convert_fusion.5), channel_id=1, source_target_pairs={{0,2},{1,3},{2,0},{3,1},{4,6},{5,7},{6,4},{7,5},{8,10},{9,11},{10,... | collective-permute-start | bytes 2359304 | tf_op jit(solution)/shard_map/ppermute | solution.py:45
  79.1 28.0 %collective-permute-start.9 = (bf16[512,768]{1,0:T(8,128)(2,1)}, bf16[512,768]{1,0:T(8,128)(2,1)}, u32[]{:S(2)}, u32[]{:S(2)}) collective-permute-start(bf16[512,768]{1,0:T(8,128)(2,1)} %add_convert_fusion.3), channel_id=1, source_target_pairs={{0,2},{1,3},{2,0},{3,1},{4,6},{5,7},{6,4},{7,5},{8,10},{9,11},{10,... | collective-permute-start | bytes 2359304 | tf_op jit(solution)/shard_map/ppermute | solution.py:45
  128.5 20.7 %collective-permute-start.13 = (bf16[512,768]{1,0:T(8,128)(2,1)}, bf16[512,768]{1,0:T(8,128)(2,1)}, u32[]{:S(2)}, u32[]{:S(2)}) collective-permute-start(bf16[512,768]{1,0:T(8,128)(2,1)} %add_convert_fusion.own), channel_id=1, source_target_pairs={{0,2},{1,3},{2,0},{3,1},{4,6},{5,7},{6,4},{7,5},{8,10},{9,11},{10,... | collective-permute-start | bytes 2359304 | tf_op jit(solution)/shard_map/ppermute | solution.py:45
  132.8 31.3 %collective-permute-start.11 = (bf16[512,768]{1,0:T(8,128)(2,1)}, bf16[512,768]{1,0:T(8,128)(2,1)}, u32[]{:S(2)}, u32[]{:S(2)}) collective-permute-start(bf16[512,768]{1,0:T(8,128)(2,1)} %add_convert_fusion.1.own), channel_id=1, source_target_pairs={{0,2},{1,3},{2,0},{3,1},{4,6},{5,7},{6,4},{7,5},{8,10},{9,11},{10,... | collective-permute-start | bytes 2359304 | tf_op jit(solution)/shard_map/ppermute | solution.py:45
  137.8 66.6 %collective-permute-start.28 = (bf16[768,768]{1,0:T(8,128)(2,1)}, bf16[768,768]{1,0:T(8,128)(2,1)}, u32[]{:S(2)}, u32[]{:S(2)}) collective-permute-start(bf16[768,768]{1,0:T(8,128)(2,1)} %fusion.47), channel_id=1, source_target_pairs={{0,1},{1,0},{2,3},{3,2},{4,5},{5,4},{6,7},{7,6},{8,9},{9,8},{10,11... | collective-permute-start | bytes 3538952 | tf_op jit(solution)/shard_map/ppermute | solution.py:45
  142.1 65.3 %collective-permute-start.32 = (bf16[768,768]{1,0:T(8,128)(2,1)}, bf16[768,768]{1,0:T(8,128)(2,1)}, u32[]{:S(2)}, u32[]{:S(2)}) collective-permute-start(bf16[768,768]{1,0:T(8,128)(2,1)} %fusion.44), channel_id=1, source_target_pairs={{0,1},{1,0},{2,3},{3,2},{4,5},{5,4},{6,7},{7,6},{8,9},{9,8},{10,11... | collective-permute-start | bytes 3538952 | tf_op jit(solution)/shard_map/ppermute | solution.py:45
  143.9 89.5 %collective-permute-start.10 = (bf16[1024,768]{1,0:T(8,128)(2,1)}, bf16[1024,768]{1,0:T(8,128)(2,1)}, u32[]{:S(2)}, u32[]{:S(2)}) collective-permute-start(bf16[1024,768]{1,0:T(8,128)(2,1)} %pad_maximum_fusion.4), channel_id=1, source_target_pairs={{0,1},{1,0},{2,3},{3,2},{4,5},{5,4},{6,7},{7,6},{8,9},{9,8},{10,11... | collective-permute-start | bytes 4718600 | tf_op jit(solution)/shard_map/ppermute | solution.py:45
  185.9 39.7 %collective-permute-start.14 = (bf16[512,768]{1,0:T(8,128)(2,1)S(1)}, bf16[512,768]{1,0:T(8,128)(2,1)S(1)}, u32[]{:S(2)}, u32[]{:S(2)}) collective-permute-start(bf16[512,768]{1,0:T(8,128)(2,1)S(1)} %copy-done.30), channel_id=1, source_target_pairs={{0,2},{1,3},{2,0},{3,1},{4,6},{5,7},{6,4},{7,5},{8,10},{9,11},{10,... | collective-permute-start | bytes 2359304 | tf_op jit(solution)/shard_map/ppermute | solution.py:45
  188.5 4.8 %collective-permute-start.16 = (bf16[8,288]{1,0:T(8,128)(2,1)S(1)}, bf16[8,288]{1,0:T(8,128)(2,1)S(1)}, u32[]{:S(2)}, u32[]{:S(2)}) collective-permute-start(bf16[8,288]{1,0:T(8,128)(2,1)S(1)} %pad_maximum_fusion.15), channel_id=1, source_target_pairs={{0,1},{1,0},{2,3},{3,2},{4,5},{5,4},{6,7},{7,6},{8,9},{9,8},{10,11... | collective-permute-start | bytes 13832 | tf_op jit(solution)/shard_map/ppermute | solution.py:45
  202.3 26.7 %collective-permute-start.12 = (bf16[512,768]{1,0:T(8,128)(2,1)}, bf16[512,768]{1,0:T(8,128)(2,1)}, u32[]{:S(2)}, u32[]{:S(2)}) collective-permute-start(bf16[512,768]{1,0:T(8,128)(2,1)} %get-tuple-element.44), channel_id=1, source_target_pairs={{0,2},{1,3},{2,0},{3,1},{4,6},{5,7},{6,4},{7,5},{8,10},{9,11},{10,... | collective-permute-start | bytes 2359304 | tf_op jit(solution)/shard_map/ppermute | solution.py:45
  204.4 32.9 %collective-permute-start.20 = (bf16[8,288,192]{2,1,0:T(8,128)(2,1)}, bf16[8,288,192]{2,1,0:T(8,128)(2,1)}, u32[]{:S(2)}, u32[]{:S(2)}) collective-permute-start(bf16[8,288,192]{2,1,0:T(8,128)(2,1)} %get-tuple-element.62), channel_id=1, source_target_pairs={{0,1},{1,0},{2,3},{3,2},{4,5},{5,4},{6,7},{7,6},{8,9},{9,8},{10,11... | collective-permute-start | bytes 2654216 | tf_op jit(solution)/shard_map/ppermute | solution.py:45
  207.4 6.3 %collective-permute-start.25 = (bf16[4,1,24,768]{3,2,0,1:T(8,128)(2,1)S(1)}, bf16[4,1,24,768]{3,2,0,1:T(8,128)(2,1)S(1)}, u32[]{:S(2)}, u32[]{:S(2)}) collective-permute-start(bf16[4,1,24,768]{3,2,0,1:T(8,128)(2,1)S(1)} %fusion.64), channel_id=1, source_target_pairs={{0,4},{4,0},{8,12},{12,8},{16,20},{20,16},{24,28},{28,24},{1,5},{5... | collective-permute-start | bytes 442376 | tf_op jit(solution)/shard_map/ppermute | solution.py:45
  213.8 4.4 %collective-permute-start.26 = (bf16[2,1,24,768]{3,2,1,0:T(8,128)(2,1)S(1)}, bf16[2,1,24,768]{3,2,1,0:T(8,128)(2,1)S(1)}, u32[]{:S(2)}, u32[]{:S(2)}) collective-permute-start(bf16[2,1,24,768]{3,2,1,0:T(8,128)(2,1)S(1)} %fusion.65), channel_id=1, source_target_pairs={{0,8},{4,12},{8,0},{12,4},{16,24},{20,28},{24,16},{28,20},{1,9},{5... | collective-permute-start | bytes 221192 | tf_op jit(solution)/shard_map/ppermute | solution.py:45
  218.3 4.9 %collective-permute-start.27 = (bf16[1,1,24,768]{3,2,1,0:T(8,128)(2,1)S(1)}, bf16[1,1,24,768]{3,2,1,0:T(8,128)(2,1)S(1)}, u32[]{:S(2)}, u32[]{:S(2)}) collective-permute-start(bf16[1,1,24,768]{3,2,1,0:T(8,128)(2,1)S(1)} %dynamic-slice_convert_fusion.7), channel_id=1, source_target_pairs={{0,16},{4,20},{8,24},{12,28},{16,0},{20,4},{24,8},{28,12},{1,17},{... | collective-permute-start | bytes 110600 | tf_op jit(solution)/shard_map/ppermute | solution.py:45
  223.2 67.9 %collective-permute-start.19 = (bf16[1,1,288]{2,0,1:T(2,128)(2,1)S(1)}, bf16[1,1,288]{2,0,1:T(2,128)(2,1)S(1)}, u32[]{:S(2)}, u32[]{:S(2)}) collective-permute-start(bf16[1,1,288]{2,0,1:T(2,128)(2,1)S(1)} %fusion.79), channel_id=1, source_target_pairs={{0,16},{4,20},{8,24},{12,28},{16,0},{20,4},{24,8},{28,12},{1,17},{... | collective-permute-start | bytes 1736 | tf_op jit(solution)/shard_map/ppermute | solution.py:45
  225.6 16.5 %collective-permute-start.29 = (bf16[4,1,96,768]{3,2,0,1:T(8,128)(2,1)}, bf16[4,1,96,768]{3,2,0,1:T(8,128)(2,1)S(1)}, u32[]{:S(2)}, u32[]{:S(2)}) collective-permute-start(bf16[4,1,96,768]{3,2,0,1:T(8,128)(2,1)} %fusion.57), channel_id=1, source_target_pairs={{0,4},{4,0},{8,12},{12,8},{16,20},{20,16},{24,28},{28,24},{1,5},{5... | collective-permute-start | bytes 1769480 | tf_op jit(solution)/shard_map/ppermute | solution.py:45
  229.0 25.7 %collective-permute-start.33 = (bf16[4,1,96,768]{3,2,0,1:T(8,128)(2,1)S(1)}, bf16[4,1,96,768]{3,2,0,1:T(8,128)(2,1)S(1)}, u32[]{:S(2)}, u32[]{:S(2)}) collective-permute-start(bf16[4,1,96,768]{3,2,0,1:T(8,128)(2,1)S(1)} %copy-done.40), channel_id=1, source_target_pairs={{0,4},{4,0},{8,12},{12,8},{16,20},{20,16},{24,28},{28,24},{1,5},{5... | collective-permute-start | bytes 1769480 | tf_op jit(solution)/shard_map/ppermute | solution.py:45
  233.4 67.7 %collective-permute-start.15 = (f32[1024,768]{1,0:T(8,128)}, f32[1024,768]{1,0:T(8,128)}, u32[]{:S(2)}, u32[]{:S(2)}) collective-permute-start(f32[1024,768]{1,0:T(8,128)} %pad_maximum_fusion.2), channel_id=1, source_target_pairs={{0,1},{1,0},{2,3},{3,2},{4,5},{5,4},{6,7},{7,6},{8,9},{9,8},{10,11... | collective-permute-start | bytes 9437192 | tf_op jit(solution)/shard_map/ppermute | solution.py:45
  240.0 26.2 %collective-permute-start.21 = (bf16[4,1,288,192]{3,2,0,1:T(8,128)(2,1)S(1)}, bf16[4,1,288,192]{3,2,0,1:T(8,128)(2,1)S(1)}, u32[]{:S(2)}, u32[]{:S(2)}) collective-permute-start(bf16[4,1,288,192]{3,2,0,1:T(8,128)(2,1)S(1)} %fusion.56), channel_id=1, source_target_pairs={{0,4},{4,0},{8,12},{12,8},{16,20},{20,16},{24,28},{28,24},{1,5},{5... | collective-permute-start | bytes 1327112 | tf_op jit(solution)/shard_map/ppermute | solution.py:45
  242.3 14.5 %collective-permute-start.30 = (bf16[2,1,96,768]{3,2,1,0:T(8,128)(2,1)S(1)}, bf16[2,1,96,768]{3,2,1,0:T(8,128)(2,1)S(1)}, u32[]{:S(2)}, u32[]{:S(2)}) collective-permute-start(bf16[2,1,96,768]{3,2,1,0:T(8,128)(2,1)S(1)} %fusion.60), channel_id=1, source_target_pairs={{0,8},{4,12},{8,0},{12,4},{16,24},{20,28},{24,16},{28,20},{1,9},{5... | collective-permute-start | bytes 884744 | tf_op jit(solution)/shard_map/ppermute | solution.py:45
  254.9 11.1 %collective-permute-start.34 = (bf16[2,1,96,768]{3,2,1,0:T(8,128)(2,1)S(1)}, bf16[2,1,96,768]{3,2,1,0:T(8,128)(2,1)S(1)}, u32[]{:S(2)}, u32[]{:S(2)}) collective-permute-start(bf16[2,1,96,768]{3,2,1,0:T(8,128)(2,1)S(1)} %fusion.61), channel_id=1, source_target_pairs={{0,8},{4,12},{8,0},{12,4},{16,24},{20,28},{24,16},{28,20},{1,9},{5... | collective-permute-start | bytes 884744 | tf_op jit(solution)/shard_map/ppermute | solution.py:45
  257.1 10.9 %collective-permute-start.31 = (bf16[1,1,96,768]{3,2,1,0:T(8,128)(2,1)S(1)}, bf16[1,1,96,768]{3,2,1,0:T(8,128)(2,1)S(1)}, u32[]{:S(2)}, u32[]{:S(2)}) collective-permute-start(bf16[1,1,96,768]{3,2,1,0:T(8,128)(2,1)S(1)} %dynamic-slice_convert_fusion.4), channel_id=1, source_target_pairs={{0,16},{4,20},{8,24},{12,28},{16,0},{20,4},{24,8},{28,12},{1,17},{... | collective-permute-start | bytes 442376 | tf_op jit(solution)/shard_map/ppermute | solution.py:45
  266.1 13.1 %collective-permute-start.35 = (bf16[1,1,96,768]{3,2,1,0:T(8,128)(2,1)S(1)}, bf16[1,1,96,768]{3,2,1,0:T(8,128)(2,1)S(1)}, u32[]{:S(2)}, u32[]{:S(2)}) collective-permute-start(bf16[1,1,96,768]{3,2,1,0:T(8,128)(2,1)S(1)} %dynamic-slice_convert_fusion.3), channel_id=1, source_target_pairs={{0,16},{4,20},{8,24},{12,28},{16,0},{20,4},{24,8},{28,12},{1,17},{... | collective-permute-start | bytes 442376 | tf_op jit(solution)/shard_map/ppermute | solution.py:45
  266.4 9.9 %collective-permute-start.22 = (bf16[2,1,288,192]{3,2,1,0:T(8,128)(2,1)S(1)}, bf16[2,1,288,192]{3,2,1,0:T(8,128)(2,1)S(1)}, u32[]{:S(2)}, u32[]{:S(2)}) collective-permute-start(bf16[2,1,288,192]{3,2,1,0:T(8,128)(2,1)S(1)} %fusion.59), channel_id=1, source_target_pairs={{0,8},{4,12},{8,0},{12,4},{16,24},{20,28},{24,16},{28,20},{1,9},{5... | collective-permute-start | bytes 663560 | tf_op jit(solution)/shard_map/ppermute | solution.py:45
  277.9 7.4 %collective-permute-start.23 = (bf16[1,1,288,192]{3,2,1,0:T(8,128)(2,1)}, bf16[1,1,288,192]{3,2,1,0:T(8,128)(2,1)}, u32[]{:S(2)}, u32[]{:S(2)}) collective-permute-start(bf16[1,1,288,192]{3,2,1,0:T(8,128)(2,1)} %dynamic-slice_convert_fusion.6), channel_id=1, source_target_pairs={{0,16},{4,20},{8,24},{12,28},{16,0},{20,4},{24,8},{28,12},{1,17},{... | collective-permute-start | bytes 331784 | tf_op jit(solution)/shard_map/ppermute | solution.py:45
  (67 other events, 458.0 us)
where the time goes:
time: 312 us; the launch traced here: 307 us
  waiting for transfers between devices  95.6 us (31%)
  other arithmetic  55.2 us (18%)
  Pallas kernels  50.5 us (16%)
  matrix products  38.4 us (12%)
  starting transfers between devices  32.1 us (10%)
  local copies, waits for them, and re-layouts  31.6 us (10%)
  between operations  3.2 us (1%)
    ppermute x36, waiting for transfers between devices, swap(): return lax.ppermute(value, axis, [(i, i ^ bit) for i in range(size)])  95.6 us
    pallas_call x5, Pallas kernels, call(): pl.pallas_call(kernel, in_specs=[SMEM if a.ndim == 1 else VMEM for a in i...  50.5 us
    ppermute x36, starting transfers between devices, swap(): return lax.ppermute(value, axis, [(i, i ^ bit) for i in range(size)])  32.1 us
    dot_general x5, matrix products, t_dot(): lax.dot_general(a, b, (((0,), (0,)), ((), ())), preferred_element_type=F32)  15.9 us
    dot_general x8, matrix products, dot(): lax.dot_general(a, b, (((1,), (0,)), ((), ())), preferred_element_type=F32)  13.1 us
    unnamed x133, local copies, waits for them, and re-layouts  12.6 us
    dot_general x8, matrix products, dot_t(): lax.dot_general(a, b, (((1,), (1,)), ((), ())), preferred_element_type=F32)  9.37 us
    add x1, other arithmetic, body(): new_average = 0.75 * average + 0.25 * new_master  9.16 us
  transfers between devices with their start and end apart: 36, of which 18 were waited for; matrix products, arithmetic and copies ran while one was open for 30% of the time, Pallas kernels for 14%

commit v1 on v0

--- a/solution.py
+++ b/solution.py
@@ -215,26 +215,18 @@
     )(*inputs)
 
 
-def scatter_sum(blocks, first, order):
-    ndata = blocks.shape[0]
-    rank = lax.axis_index("dp")
-    cur = blocks[None]
-    left = list(range(ndata.bit_length() - 1))
-    for bit in order(left):
-        low = sum(1 for b in left if b < bit)
-        rest = cur.shape[2:]
-        view = cur.reshape((cur.shape[1] >> (low + 1), 2, 1 << low) + rest)
-        mine = (rank >> bit) & 1
-        keep = lax.dynamic_index_in_dim(view, mine, 1, keepdims=False)
-        send = lax.dynamic_index_in_dim(view, 1 - mine, 1, keepdims=False)
-        got = swap(send.astype(BF), "dp", 1 << bit)
-        cur = (keep.astype(F32) + got.astype(F32)).reshape((1, -1) + rest)
-        left.remove(bit)
-    return cur[0, 0]
-
-
-def upward(left):
-    return list(left)
+def scatter_step(cur, bit):
+    mine = (lax.axis_index("dp") >> bit) & 1
+    view = cur.reshape((-1, 2) + cur.shape[1:])
+    keep = lax.dynamic_index_in_dim(view, mine, 1, keepdims=False)
+    send = lax.dynamic_index_in_dim(view, 1 - mine, 1, keepdims=False)
+    return keep.astype(F32) + swap(send.astype(BF), "dp", 1 << bit).astype(F32)
+
+
+def scatter_sum(blocks, first=0):
+    for bit in range(first, lax.axis_size("dp").bit_length() - 1):
+        blocks = scatter_step(blocks, bit)
+    return blocks[0]
 
 
 def body(
@@ -334,7 +326,7 @@
         act = struct((SLOT_TOKENS, wide), BF)
         dz, dzb, dq, dk, dv, sums, back = call(
             backward_kernel,
-            (info[i], third[0], part, other, normed, rstd, vec[0:1], q, k, v, ctx, lse, w_attn, wo),
+            (info[i], third, part, other, normed, rstd, vec[0:1], q, k, v, ctx, lse, w_attn, wo),
             (
                 struct((SLOT_TOKENS, model), F32),
                 struct((SLOT_TOKENS, model), BF),
@@ -357,19 +349,6 @@
     two_r = [across(two[i][1]) for i in n]
     three = [phase_three(i, two[i][0], two[i][1], two_r[i]) for i in n]
     three_r = [across(three[i][2]) for i in n]
-    four = [phase_four(i, one[i][0], two[i][0], three[i][1], three[i][2], three_r[i]) for i in n]
-    four_r = [across(four[i][1]) for i in n]
-
-    def whole(half, other):
-        first = jnp.where(core == 0, half, other)
-        second = jnp.where(core == 0, other, half)
-        return jnp.concatenate([first, second])
-
-    out_half = jnp.concatenate([three[i][0] for i in n])
-    output = whole(out_half, swap(out_half, "mp", 1))
-    gi_half = jnp.concatenate([four[i][0][0] + total(four[i][1], four_r[i]) for i in n])
-    grad_input = whole(gi_half, swap(gi_half, "mp", 1))
-
     def over_cores(parts):
         return parts[0] + swap(parts[1].astype(BF), "mp", 1).astype(F32)
 
@@ -382,15 +361,32 @@
         g_down.append(t_dot(cat(lambda i: two[i][0][4][g]), dz2_all))
         g_in.append(t_dot(xb_all, dpre))
         g_inb.append(jnp.sum(dpre.astype(F32), axis=0))
-    s_down = scatter_sum(over_cores(g_down).reshape(ndata, -1, g_down[0].shape[1]), None, upward)
-    s_in = scatter_sum(over_cores(g_in).reshape(ndata, -1, g_in[0].shape[1]), None, upward)
+    ffn = [over_cores(g).reshape(ndata, -1, model) for g in (g_in, g_down)]
+    dz_two = [three[i][1][0] for i in n]
+    dz_two[0], *ffn = lax.optimization_barrier((dz_two[0], *ffn))
+    ffn = [scatter_step(t, 0) for t in ffn]
+
+    four = [phase_four(i, one[i][0], two[i][0], dz_two[i], three[i][2], three_r[i]) for i in n]
+    four_r = [across(four[i][1]) for i in n]
+
+    def whole(half, other):
+        first = jnp.where(core == 0, half, other)
+        second = jnp.where(core == 0, other, half)
+        return jnp.concatenate([first, second])
+
+    out_half = jnp.concatenate([three[i][0] for i in n])
+    output = whole(out_half, swap(out_half, "mp", 1))
+    gi_half = jnp.concatenate([four[i][0][0] + total(four[i][1], four_r[i]) for i in n])
+    grad_input = whole(gi_half, swap(gi_half, "mp", 1))
 
     ctx_all = cat(lambda i: one[i][0][3])
     dz1_all = cat(lambda i: four[i][0][1])
     g_full = t_dot(ctx_all, dz1_all)
     g_out = [g_full[:cols], g_full[cols:]]
-    s_out = scatter_sum(over_cores(g_out).reshape(ndata, -1, model), None, upward)
+    s_out = scatter_sum(over_cores(g_out).reshape(ndata, -1, model))
     pairs = [four[i][0][2][t] for t in range(3) for i in n]
+    pairs[0], *ffn = lax.optimization_barrier((pairs[0], *ffn))
+    s_in, s_down = (scatter_sum(t, 1) for t in ffn)
     block = (ndata, 3 * model // ndata, cols)
     g_own, g_other, g_sums = call(
         lambda *refs: gradient_kernel(ndata, *refs),
@@ -399,7 +395,7 @@
         flops=6 * slot_flops,
         name="attn_grad",
     )
-    s_qkv = scatter_sum(g_own + swap(g_other, "mp", 1).astype(F32), None, upward)
+    s_qkv = scatter_sum(g_own + swap(g_other, "mp", 1).astype(F32))
     g_col = [jnp.stack([g_sums[0, c], g_sums[2, c]]) for c in (slice(0, cols), slice(cols, wide))]
 
     add = lambda t: sum(t[1:], t[0])
@@ -413,7 +409,7 @@
         small.append(
             jnp.concatenate([g_col[g].reshape(ndata, -1), g_inb[g].reshape(ndata, -1), share.reshape(ndata, -1)], axis=1)
         )
-    s_small = scatter_sum(over_cores(small), None, upward)
+    s_small = scatter_sum(over_cores(small))
     n_vec = g_vec.shape[1] // ndata
 
     grad = jnp.concatenate([s_qkv.reshape(-1), s_out.reshape(-1), s_in.reshape(-1), s_down.reshape(-1), s_small])

time: 312 us -> 329 us (1.054)
  waiting for transfers between devices: 95.6 us -> 106 us
  other arithmetic: 55.2 us -> 60.5 us
    ppermute x36, waiting for transfers between devices: 95.6 us -> 106 us  [swap(): return lax.ppermute(value, axis, [(i, i ^ bit) for i in range(size)])]
    add x15, other arithmetic: 5.03 us -> 10.8 us  [the longest x14 9.13 us: scatter_step(): return keep.astype(F32) + swap(send.astype(BF), 'dp', 1 << bit).astype(F32)]
    unnamed x133 -> x117, local copies, waits for them, and re-layouts: 12.6 us -> 11 us
  transfers between devices with their start and end apart: 36 -> 36, of which waited for: 18 -> 14; matrix products, arithmetic and copies ran while one was open for 30% -> 33% of each run, Pallas kernels for 14% -> 13%
where the time goes in v1:
time: 329 us; the launch traced here: 323 us
  waiting for transfers between devices  106 us (32%)
  other arithmetic  60.5 us (18%)
  Pallas kernels  51.3 us (16%)
  matrix products  38.4 us (12%)
  local copies, waits for them, and re-layouts  32.6 us (10%)
  starting transfers between devices  31.5 us (10%)
    ppermute x36, waiting for transfers between devices, swap(): return lax.ppermute(value, axis, [(i, i ^ bit) for i in range(size)])  106 us
    pallas_call x5, Pallas kernels, call(): pl.pallas_call(kernel, in_specs=[SMEM if a.ndim == 1 else VMEM for a in i...  51.3 us
    ppermute x36, starting transfers between devices, swap(): return lax.ppermute(value, axis, [(i, i ^ bit) for i in range(size)])  31.5 us
    dot_general x5, matrix products, t_dot(): lax.dot_general(a, b, (((0,), (0,)), ((), ())), preferred_element_type=F32)  16 us
    dot_general x8, matrix products, dot(): lax.dot_general(a, b, (((1,), (0,)), ((), ())), preferred_element_type=F32)  13 us
    unnamed x117, local copies, waits for them, and re-layouts  11 us
    add x1, other arithmetic, body(): new_average = 0.75 * average + 0.25 * new_master  9.46 us
    dot_general x8, matrix products, dot_t(): lax.dot_general(a, b, (((1,), (1,)), ((), ())), preferred_element_type=F32)  9.33 us
  transfers between devices with their start and end apart: 36, of which 14 were waited for; matrix products, arithmetic and copies ran while one was open for 33% of the time, Pallas kernels for 13%

profile of v1, /device:TPU:0, one launch (start us, length us, event | category | flops | bytes accessed | tf_op | source)
XLA Modules:
  0.0 323.3 jit_solution(15915579549460591579)
XLA Ops:
  4.7 2.7 constant_dynamic-slice_fusion
  12.1 8.0 %attn_fwd.2 = (bf16[512,384]{1,0:T(8,128)(2,1)}, bf16[512,384]{1,0:T(8,128)(2,1)}, bf16[512,384]{1,0:T(8,128)(2,1)}, bf16[512,384]{1,0:T(8,128)(2,1)}, f32[512,384]{1,0:T(8,128)}, /*index=5*/bf16[512,768]{1,0:T(8,128)(2,1)}) custom-call(s32[5]{0:T(128)} %pad_add_fusion.info, bf16[512,768]{1,0:T(8,128)(2,1)} %get-tuple-element.127.x, ...), custom_call_target="tpu_custom_call" | custom-call | flops 1811939328 | bytes 6294548 | tf_op jit(solution)/shard_map/attn_fwd/pallas_call | solution.py:207
  20.1 2.6 collective-permute-start.3
  22.7 8.7 %attn_fwd.3 = (bf16[512,384]{1,0:T(8,128)(2,1)}, bf16[512,384]{1,0:T(8,128)(2,1)}, bf16[512,384]{1,0:T(8,128)(2,1)}, bf16[512,384]{1,0:T(8,128)(2,1)}, f32[512,384]{1,0:T(8,128)}, /*index=5*/bf16[512,768]{1,0:T(8,128)(2,1)}) custom-call(s32[5]{0:T(128)} %pad_add_fusion.1.info, bf16[512,768]{1,0:T(8,128)(2,1)} %get-tuple-element.126.x, ...), custom_call_target="tpu_custom_call" | custom-call | flops 1811939328 | bytes 6294548 | tf_op jit(solution)/shard_map/attn_fwd/pallas_call | solution.py:207
  32.2 2.3 collective-permute-done.5
  34.5 6.8 %collective-permute-done.3 = bf16[512,768]{1,0:T(8,128)(2,1)S(1)} collective-permute-done((bf16[512,768]{1,0:T(8,128)(2,1)}, bf16[512,768]{1,0:T(8,128)(2,1)S(1)}, u32[]{:S(2)}, u32[]{:S(2)}) %collective-permute-start.3) | collective-permute-done | bytes 786464 | tf_op jit(solution)/shard_map/ppermute | solution.py:45
  41.3 16.6 %collective-permute-done.8 = bf16[512,768]{1,0:T(8,128)(2,1)S(1)} collective-permute-done((bf16[512,768]{1,0:T(8,128)(2,1)}, bf16[512,768]{1,0:T(8,128)(2,1)S(1)}, u32[]{:S(2)}, u32[]{:S(2)}) %collective-permute-start.8) | collective-permute-done | bytes 786464 | tf_op jit(solution)/shard_map/ppermute | solution.py:45
  61.0 2.8 fusion.50
  82.1 2.8 constant_dynamic-slice_fusion.11.refs_0_
  87.8 3.5 %collective-permute-done.9 = bf16[512,768]{1,0:T(8,128)(2,1)} collective-permute-done((bf16[512,768]{1,0:T(8,128)(2,1)}, bf16[512,768]{1,0:T(8,128)(2,1)}, u32[]{:S(2)}, u32[]{:S(2)}) %collective-permute-start.9) | collective-permute-done | bytes 786464 | tf_op jit(solution)/shard_map/ppermute | solution.py:45
  91.3 15.7 %collective-permute-done.7 = bf16[512,768]{1,0:T(8,128)(2,1)} collective-permute-done((bf16[512,768]{1,0:T(8,128)(2,1)}, bf16[512,768]{1,0:T(8,128)(2,1)}, u32[]{:S(2)}, u32[]{:S(2)}) %collective-permute-start.7) | collective-permute-done | bytes 786464 | tf_op jit(solution)/shard_map/ppermute | solution.py:45
  107.1 2.8 fusion.89
  118.0 2.5 fusion.44
  123.3 2.6 fusion.47
  140.0 13.0 %collective-permute-done.15.other = bf16[512,768]{1,0:T(8,128)(2,1)} collective-permute-done((bf16[512,768]{1,0:T(8,128)(2,1)}, bf16[512,768]{1,0:T(8,128)(2,1)}, u32[]{:S(2)}, u32[]{:S(2)}) %collective-permute-start.15) | collective-permute-done | bytes 786464 | tf_op jit(solution)/shard_map/ppermute | solution.py:45
  153.1 13.8 %attn_bwd.3 = (f32[512,768]{1,0:T(8,128)}, bf16[512,768]{1,0:T(8,128)(2,1)}, bf16[512,384]{1,0:T(8,128)(2,1)}, bf16[512,384]{1,0:T(8,128)(2,1)}, bf16[512,384]{1...) custom-call(s32[5]{0:T(128)} %pad_add_fusion.1.info, f32[512,768]{1,0:T(8,128)} %copy-done.7, ...), custom_call_target="tpu_custom_call" | custom-call | flops 3019898880 | bytes 13792276 | tf_op jit(solution)/shard_map/attn_bwd/pallas_call | solution.py:207
  168.4 3.7 %convert_add_fusion.1 = f32[768,768]{1,0:T(8,128)S(1)} fusion(bf16[768,768]{1,0:T(8,128)(2,1)} %collective-permute-done.12, bf16[512,768]{1,0:T(8,128)(2,1)} %copy-done.48, bf16[512,768]{1,0:T(8,128)(2,1)} %copy-done.49, bf16[512,768]{1,0:T(8,128)(2,1)} %copy-done.31, bf16[512,768]{1,0:T(8,128)(2,1)} %copy-done.30), kind=kOutput, calls=%fused_computation.9 | convolution fusion | flops 1215430656 | bytes 6684672 | tf_op jit(solution)/shard_map/dot_general | solution.py:40
  172.1 5.0 %convert_add_fusion.2 = f32[768,768]{1,0:T(8,128)} fusion(bf16[768,768]{1,0:T(8,128)(2,1)} %collective-permute-done.11, bf16[512,768]{1,0:T(8,128)(2,1)S(1)} %copy-done.29, bf16[512,768]{1,0:T(8,128)(2,1)S(1)} %copy-done.27, bf16[512,768]{1,0:T(8,128)(2,1)S(1)} %copy-done.25, bf16[512,768]{1,0:T(8,128)(2,1)S(1)} %copy-done.23), kind=kOutput, calls=%fused_computation.10 | convolution fusion | flops 1215430656 | bytes 6684672 | tf_op jit(solution)/shard_map/dot_general | solution.py:40
  179.5 13.9 %attn_bwd.2 = (f32[512,768]{1,0:T(8,128)}, bf16[512,768]{1,0:T(8,128)(2,1)}, bf16[512,384]{1,0:T(8,128)(2,1)}, bf16[512,384]{1,0:T(8,128)(2,1)}, bf16[512,384]{1...) custom-call(s32[5]{0:T(128)} %pad_add_fusion.info, f32[512,768]{1,0:T(8,128)} %copy-done.6, ...), custom_call_target="tpu_custom_call" | custom-call | flops 3019898880 | bytes 13792276 | tf_op jit(solution)/shard_map/attn_bwd/pallas_call | solution.py:207
  204.0 13.0 %collective-permute-done.29 = bf16[4,24,768]{2,1,0:T(8,128)(2,1)S(1)} collective-permute-done((bf16[4,24,768]{2,1,0:T(8,128)(2,1)S(1)}, bf16[4,24,768]{2,1,0:T(8,128)(2,1)S(1)}, u32[]{:S(2)}, u32[]{:S(2)}) %collective-permute-start.29) | collective-permute-done | bytes 147488 | tf_op jit(solution)/shard_map/ppermute | solution.py:45
  221.6 2.7 collective-permute-start.31
  226.6 2.7 bitcast_add_fusion.1
  230.6 7.0 %attn_grad.1 = (f32[8,288,192]{2,1,0:T(8,128)}, bf16[8,288,192]{2,1,0:T(8,128)(2,1)}, f32[8,384]{1,0:T(8,128)}) custom-call(bf16[1024,768]{1,0:T(8,128)(2,1)} %constant_dynamic-slice_fusion.11.refs_0_, bf16[512,384]{1,0:T(8,128)(2,1)} %get-tuple-element.62.refs_1_, bf16[512,384]{1,0:T(8,128)(2,1)} %get-tuple-element.63.refs_2_, ...), custom_call_target="tpu_custom_call" | custom-call | flops 1811939328 | bytes 6598656 | tf_op jit(solution)/shard_map/attn_grad/pallas_call | solution.py:207
  244.1 3.0 collective-permute-done.21
  248.8 8.4 %collective-permute-done.22 = bf16[2,288]{1,0:T(2,128)(2,1)S(1)} collective-permute-done((bf16[2,288]{1,0:T(2,128)(2,1)S(1)}, bf16[2,288]{1,0:T(2,128)(2,1)S(1)}, u32[]{:S(2)}, u32[]{:S(2)}) %collective-permute-start.22) | collective-permute-done | bytes 1184 | tf_op jit(solution)/shard_map/ppermute | solution.py:45
  257.3 2.8 collective-permute-start.23
  269.3 2.5 collective-permute-start.33
  271.8 10.8 %collective-permute-done.25 = bf16[4,288,192]{2,1,0:T(8,128)(2,1)S(1)} collective-permute-done((bf16[4,288,192]{2,1,0:T(8,128)(2,1)S(1)}, bf16[4,288,192]{2,1,0:T(8,128)(2,1)S(1)}, u32[]{:S(2)}, u32[]{:S(2)}) %collective-permute-start.25) | collective-permute-done | bytes 442400 | tf_op jit(solution)/shard_map/ppermute | solution.py:45
  284.7 6.5 %collective-permute-done.26 = bf16[2,288,192]{2,1,0:T(8,128)(2,1)S(1)} collective-permute-done((bf16[2,288,192]{2,1,0:T(8,128)(2,1)S(1)}, bf16[2,288,192]{2,1,0:T(8,128)(2,1)S(1)}, u32[]{:S(2)}, u32[]{:S(2)}) %collective-permute-start.26) | collective-permute-done | bytes 221216 | tf_op jit(solution)/shard_map/ppermute | solution.py:45
  296.7 4.6 %collective-permute-done.27 = bf16[1,288,192]{2,1,0:T(8,128)(2,1)} collective-permute-done((bf16[1,288,192]{2,1,0:T(8,128)(2,1)}, bf16[1,288,192]{2,1,0:T(8,128)(2,1)}, u32[]{:S(2)}, u32[]{:S(2)}) %collective-permute-start.27) | collective-permute-done | bytes 110624 | tf_op jit(solution)/shard_map/ppermute | solution.py:45
  307.3 9.5 %multiply_add_fusion.2 = (f32[1,1,221472]{2,1,0:T(1,128)}, f32[1,1,221472]{2,1,0:T(1,128)}, f32[1,1,221472]{2,1,0:T(1,128)}, f32[1,1,221472]{2,1,0:T(1,128)}) fusion(f32[1,1,221472]{2,1,0:T(1,128)S(1)} %copy-done.19, f32[1,1,221472]{2,1,0:T(1,128)S(1)} %copy-done.20, f32[1,1,221472]{2,1,0:T(1,128)S(1)} %get-tuple-element.106, f32[1,1,221472]{2,1,0:T(1,128)} %param.27, ...), kind=kLoop, calls=%fused_computation.119 | loop fusion | flops 3986496 | bytes 7972992 | tf_op jit(solution)/shard_map/add | solution.py:424
  319.7 3.1 pad_maximum_fusion
  (302 shorter events, 113.6 us)
Async XLA Ops:
  0.6 10.1 %collective-permute-start = (bf16[3,192,768]{2,1,0:T(8,128)(2,1)}, bf16[3,192,768]{2,1,0:T(8,128)(2,1)S(1)}, u32[]{:S(2)}, u32[]{:S(2)}) collective-permute-start(bf16[3,192,768]{2,1,0:T(8,128)(2,1)} %bitcast.126), channel_id=1, source_target_pairs={{0,1},{1,0},{2,3},{3,2},{4,5},{5,4},{6,7},{7,6},{8,9},{9,8},{10,11... | collective-permute-start | bytes 2654216 | tf_op jit(solution)/shard_map/ppermute | solution.py:45
  1.2 9.5 %collective-permute-start.2 = (bf16[192,768]{1,0:T(8,128)(2,1)}, bf16[192,768]{1,0:T(8,128)(2,1)S(1)}, u32[]{:S(2)}, u32[]{:S(2)}) collective-permute-start(bf16[192,768]{1,0:T(8,128)(2,1)} %param.19), channel_id=1, source_target_pairs={{0,1},{1,0},{2,3},{3,2},{4,5},{5,4},{6,7},{7,6},{8,9},{9,8},{10,11... | collective-permute-start | bytes 884744 | tf_op jit(solution)/shard_map/ppermute | solution.py:45
  1.3 8.7 %collective-permute-start.1 = (bf16[2,192]{1,0:T(2,128)(2,1)}, bf16[2,192]{1,0:T(2,128)(2,1)S(1)}, u32[]{:S(2)}, u32[]{:S(2)}) collective-permute-start(bf16[2,192]{1,0:T(2,128)(2,1)} %param.18), channel_id=1, source_target_pairs={{0,1},{1,0},{2,3},{3,2},{4,5},{5,4},{6,7},{7,6},{8,9},{9,8},{10,11... | collective-permute-start | bytes 2312 | tf_op jit(solution)/shard_map/ppermute | solution.py:45
  20.1 21.2 %collective-permute-start.3 = (bf16[512,768]{1,0:T(8,128)(2,1)}, bf16[512,768]{1,0:T(8,128)(2,1)S(1)}, u32[]{:S(2)}, u32[]{:S(2)}) collective-permute-start(bf16[512,768]{1,0:T(8,128)(2,1)} %get-tuple-element.42), channel_id=1, source_target_pairs={{0,2},{1,3},{2,0},{3,1},{4,6},{5,7},{6,4},{7,5},{8,10},{9,11},{10,... | collective-permute-start | bytes 2359304 | tf_op jit(solution)/shard_map/ppermute | solution.py:45
  31.4 26.5 %collective-permute-start.8 = (bf16[512,768]{1,0:T(8,128)(2,1)}, bf16[512,768]{1,0:T(8,128)(2,1)S(1)}, u32[]{:S(2)}, u32[]{:S(2)}) collective-permute-start(bf16[512,768]{1,0:T(8,128)(2,1)} %get-tuple-element.43), channel_id=1, source_target_pairs={{0,2},{1,3},{2,0},{3,1},{4,6},{5,7},{6,4},{7,5},{8,10},{9,11},{10,... | collective-permute-start | bytes 2359304 | tf_op jit(solution)/shard_map/ppermute | solution.py:45
  31.4 35.5 %collective-permute-start.4 = (bf16[768,768]{1,0:T(8,128)(2,1)}, bf16[768,768]{1,0:T(8,128)(2,1)S(1)}, u32[]{:S(2)}, u32[]{:S(2)}) collective-permute-start(bf16[768,768]{1,0:T(8,128)(2,1)} %param.20), channel_id=1, source_target_pairs={{0,1},{1,0},{2,3},{3,2},{4,5},{5,4},{6,7},{7,6},{8,9},{9,8},{10,11... | collective-permute-start | bytes 3538952 | tf_op jit(solution)/shard_map/ppermute | solution.py:45
  31.9 37.0 %collective-permute-start.6 = (bf16[768,768]{1,0:T(8,128)(2,1)}, bf16[768,768]{1,0:T(8,128)(2,1)S(1)}, u32[]{:S(2)}, u32[]{:S(2)}) collective-permute-start(bf16[768,768]{1,0:T(8,128)(2,1)} %param.22), channel_id=1, source_target_pairs={{0,1},{1,0},{2,3},{3,2},{4,5},{5,4},{6,7},{7,6},{8,9},{9,8},{10,11... | collective-permute-start | bytes 3538952 | tf_op jit(solution)/shard_map/ppermute | solution.py:45
  70.6 20.7 %collective-permute-start.9 = (bf16[512,768]{1,0:T(8,128)(2,1)}, bf16[512,768]{1,0:T(8,128)(2,1)}, u32[]{:S(2)}, u32[]{:S(2)}) collective-permute-start(bf16[512,768]{1,0:T(8,128)(2,1)} %add_convert_fusion.3), channel_id=1, source_target_pairs={{0,2},{1,3},{2,0},{3,1},{4,6},{5,7},{6,4},{7,5},{8,10},{9,11},{10,... | collective-permute-start | bytes 2359304 | tf_op jit(solution)/shard_map/ppermute | solution.py:45
  79.8 27.3 %collective-permute-start.7 = (bf16[512,768]{1,0:T(8,128)(2,1)}, bf16[512,768]{1,0:T(8,128)(2,1)}, u32[]{:S(2)}, u32[]{:S(2)}) collective-permute-start(bf16[512,768]{1,0:T(8,128)(2,1)} %add_convert_fusion.5), channel_id=1, source_target_pairs={{0,2},{1,3},{2,0},{3,1},{4,6},{5,7},{6,4},{7,5},{8,10},{9,11},{10,... | collective-permute-start | bytes 2359304 | tf_op jit(solution)/shard_map/ppermute | solution.py:45
  120.5 47.9 %collective-permute-start.12 = (bf16[768,768]{1,0:T(8,128)(2,1)}, bf16[768,768]{1,0:T(8,128)(2,1)}, u32[]{:S(2)}, u32[]{:S(2)}) collective-permute-start(bf16[768,768]{1,0:T(8,128)(2,1)} %fusion.44), channel_id=1, source_target_pairs={{0,1},{1,0},{2,3},{3,2},{4,5},{5,4},{6,7},{7,6},{8,9},{9,8},{10,11... | collective-permute-start | bytes 3538952 | tf_op jit(solution)/shard_map/ppermute | solution.py:45
  125.9 46.2 %collective-permute-start.11 = (bf16[768,768]{1,0:T(8,128)(2,1)}, bf16[768,768]{1,0:T(8,128)(2,1)}, u32[]{:S(2)}, u32[]{:S(2)}) collective-permute-start(bf16[768,768]{1,0:T(8,128)(2,1)} %fusion.47), channel_id=1, source_target_pairs={{0,1},{1,0},{2,3},{3,2},{4,5},{5,4},{6,7},{7,6},{8,9},{9,8},{10,11... | collective-permute-start | bytes 3538952 | tf_op jit(solution)/shard_map/ppermute | solution.py:45
  132.3 20.7 %collective-permute-start.15 = (bf16[512,768]{1,0:T(8,128)(2,1)}, bf16[512,768]{1,0:T(8,128)(2,1)}, u32[]{:S(2)}, u32[]{:S(2)}) collective-permute-start(bf16[512,768]{1,0:T(8,128)(2,1)} %add_convert_fusion.own), channel_id=1, source_target_pairs={{0,2},{1,3},{2,0},{3,1},{4,6},{5,7},{6,4},{7,5},{8,10},{9,11},{10,... | collective-permute-start | bytes 2359304 | tf_op jit(solution)/shard_map/ppermute | solution.py:45
  136.3 43.2 %collective-permute-start.13 = (bf16[512,768]{1,0:T(8,128)(2,1)}, bf16[512,768]{1,0:T(8,128)(2,1)}, u32[]{:S(2)}, u32[]{:S(2)}) collective-permute-start(bf16[512,768]{1,0:T(8,128)(2,1)} %add_convert_fusion.1.own), channel_id=1, source_target_pairs={{0,2},{1,3},{2,0},{3,1},{4,6},{5,7},{6,4},{7,5},{8,10},{9,11},{10,... | collective-permute-start | bytes 2359304 | tf_op jit(solution)/shard_map/ppermute | solution.py:45
  140.0 78.8 %collective-permute-start.10 = (bf16[1024,768]{1,0:T(8,128)(2,1)}, bf16[1024,768]{1,0:T(8,128)(2,1)}, u32[]{:S(2)}, u32[]{:S(2)}) collective-permute-start(bf16[1024,768]{1,0:T(8,128)(2,1)} %pad_maximum_fusion.4), channel_id=1, source_target_pairs={{0,1},{1,0},{2,3},{3,2},{4,5},{5,4},{6,7},{7,6},{8,9},{9,8},{10,11... | collective-permute-start | bytes 4718600 | tf_op jit(solution)/shard_map/ppermute | solution.py:45
  166.8 33.6 %collective-permute-start.16 = (bf16[512,768]{1,0:T(8,128)(2,1)}, bf16[512,768]{1,0:T(8,128)(2,1)}, u32[]{:S(2)}, u32[]{:S(2)}) collective-permute-start(bf16[512,768]{1,0:T(8,128)(2,1)} %get-tuple-element.58), channel_id=1, source_target_pairs={{0,2},{1,3},{2,0},{3,1},{4,6},{5,7},{6,4},{7,5},{8,10},{9,11},{10,... | collective-permute-start | bytes 2359304 | tf_op jit(solution)/shard_map/ppermute | solution.py:45
  178.0 48.6 %collective-permute-start.19 = (bf16[4,96,768]{2,1,0:T(8,128)(2,1)}, bf16[4,96,768]{2,1,0:T(8,128)(2,1)}, u32[]{:S(2)}, u32[]{:S(2)}) collective-permute-start(bf16[4,96,768]{2,1,0:T(8,128)(2,1)} %fusion.57), channel_id=1, source_target_pairs={{0,4},{4,0},{8,12},{12,8},{16,20},{20,16},{24,28},{28,24},{1,5},{5... | collective-permute-start | bytes 1769480 | tf_op jit(solution)/shard_map/ppermute | solution.py:45
  198.0 31.4 %collective-permute-start.18 = (bf16[4,96,768]{2,1,0:T(8,128)(2,1)}, bf16[4,96,768]{2,1,0:T(8,128)(2,1)}, u32[]{:S(2)}, u32[]{:S(2)}) collective-permute-start(bf16[4,96,768]{2,1,0:T(8,128)(2,1)} %fusion.56), channel_id=1, source_target_pairs={{0,4},{4,0},{8,12},{12,8},{16,20},{20,16},{24,28},{28,24},{1,5},{5... | collective-permute-start | bytes 1769480 | tf_op jit(solution)/shard_map/ppermute | solution.py:45
  199.8 60.3 %collective-permute-start.14 = (bf16[512,768]{1,0:T(8,128)(2,1)}, bf16[512,768]{1,0:T(8,128)(2,1)}, u32[]{:S(2)}, u32[]{:S(2)}) collective-permute-start(bf16[512,768]{1,0:T(8,128)(2,1)} %get-tuple-element.51), channel_id=1, source_target_pairs={{0,2},{1,3},{2,0},{3,1},{4,6},{5,7},{6,4},{7,5},{8,10},{9,11},{10,... | collective-permute-start | bytes 2359304 | tf_op jit(solution)/shard_map/ppermute | solution.py:45
  200.5 16.6 %collective-permute-start.29 = (bf16[4,24,768]{2,1,0:T(8,128)(2,1)S(1)}, bf16[4,24,768]{2,1,0:T(8,128)(2,1)S(1)}, u32[]{:S(2)}, u32[]{:S(2)}) collective-permute-start(bf16[4,24,768]{2,1,0:T(8,128)(2,1)S(1)} %fusion.64), channel_id=1, source_target_pairs={{0,4},{4,0},{8,12},{12,8},{16,20},{20,16},{24,28},{28,24},{1,5},{5... | collective-permute-start | bytes 442376 | tf_op jit(solution)/shard_map/ppermute | solution.py:45
  217.1 4.4 %collective-permute-start.30 = (bf16[2,24,768]{2,1,0:T(8,128)(2,1)S(1)}, bf16[2,24,768]{2,1,0:T(8,128)(2,1)S(1)}, u32[]{:S(2)}, u32[]{:S(2)}) collective-permute-start(bf16[2,24,768]{2,1,0:T(8,128)(2,1)S(1)} %fusion.65), channel_id=1, source_target_pairs={{0,8},{4,12},{8,0},{12,4},{16,24},{20,28},{24,16},{28,20},{1,9},{5... | collective-permute-start | bytes 221192 | tf_op jit(solution)/shard_map/ppermute | solution.py:45
  221.6 4.9 %collective-permute-start.31 = (bf16[1,24,768]{2,1,0:T(8,128)(2,1)S(1)}, bf16[1,24,768]{2,1,0:T(8,128)(2,1)S(1)}, u32[]{:S(2)}, u32[]{:S(2)}) collective-permute-start(bf16[1,24,768]{2,1,0:T(8,128)(2,1)S(1)} %dynamic-slice_convert_fusion.9), channel_id=1, source_target_pairs={{0,16},{4,20},{8,24},{12,28},{16,0},{20,4},{24,8},{28,12},{1,17},{... | collective-permute-start | bytes 110600 | tf_op jit(solution)/shard_map/ppermute | solution.py:45
  241.2 22.8 %collective-permute-start.34 = (bf16[2,96,768]{2,1,0:T(8,128)(2,1)}, bf16[2,96,768]{2,1,0:T(8,128)(2,1)}, u32[]{:S(2)}, u32[]{:S(2)}) collective-permute-start(bf16[2,96,768]{2,1,0:T(8,128)(2,1)} %fusion.60), channel_id=1, source_target_pairs={{0,8},{4,12},{8,0},{12,4},{16,24},{20,28},{24,16},{28,20},{1,9},{5... | collective-permute-start | bytes 884744 | tf_op jit(solution)/shard_map/ppermute | solution.py:45
  242.8 25.2 %collective-permute-start.32 = (bf16[2,96,768]{2,1,0:T(8,128)(2,1)S(1)}, bf16[2,96,768]{2,1,0:T(8,128)(2,1)}, u32[]{:S(2)}, u32[]{:S(2)}) collective-permute-start(bf16[2,96,768]{2,1,0:T(8,128)(2,1)S(1)} %fusion.59), channel_id=1, source_target_pairs={{0,8},{4,12},{8,0},{12,4},{16,24},{20,28},{24,16},{28,20},{1,9},{5... | collective-permute-start | bytes 884744 | tf_op jit(solution)/shard_map/ppermute | solution.py:45
  243.4 22.0 %collective-permute-start.24 = (bf16[8,288,192]{2,1,0:T(8,128)(2,1)}, bf16[8,288,192]{2,1,0:T(8,128)(2,1)}, u32[]{:S(2)}, u32[]{:S(2)}) collective-permute-start(bf16[8,288,192]{2,1,0:T(8,128)(2,1)} %get-tuple-element.72), channel_id=1, source_target_pairs={{0,1},{1,0},{2,3},{3,2},{4,5},{5,4},{6,7},{7,6},{8,9},{9,8},{10,11... | collective-permute-start | bytes 2654216 | tf_op jit(solution)/shard_map/ppermute | solution.py:45
  247.2 10.1 %collective-permute-start.22 = (bf16[2,288]{1,0:T(2,128)(2,1)S(1)}, bf16[2,288]{1,0:T(2,128)(2,1)S(1)}, u32[]{:S(2)}, u32[]{:S(2)}) collective-permute-start(bf16[2,288]{1,0:T(2,128)(2,1)S(1)} %bitcast.131), channel_id=1, source_target_pairs={{0,8},{4,12},{8,0},{12,4},{16,24},{20,28},{24,16},{28,20},{1,9},{5... | collective-permute-start | bytes 3464 | tf_op jit(solution)/shard_map/ppermute | solution.py:45
  257.3 49.9 %collective-permute-start.23 = (bf16[1,288]{1,0:T(2,128)(2,1)S(1)}, bf16[1,288]{1,0:T(2,128)(2,1)S(1)}, u32[]{:S(2)}, u32[]{:S(2)}) collective-permute-start(bf16[1,288]{1,0:T(2,128)(2,1)S(1)} %fusion.79), channel_id=1, source_target_pairs={{0,16},{4,20},{8,24},{12,28},{16,0},{20,4},{24,8},{28,12},{1,17},{... | collective-permute-start | bytes 1736 | tf_op jit(solution)/shard_map/ppermute | solution.py:45
  264.0 53.3 %collective-permute-start.17 = (f32[1024,768]{1,0:T(8,128)}, f32[1024,768]{1,0:T(8,128)}, u32[]{:S(2)}, u32[]{:S(2)}) collective-permute-start(f32[1024,768]{1,0:T(8,128)} %pad_maximum_fusion.2), channel_id=1, source_target_pairs={{0,1},{1,0},{2,3},{3,2},{4,5},{5,4},{6,7},{7,6},{8,9},{9,8},{10,11... | collective-permute-start | bytes 9437192 | tf_op jit(solution)/shard_map/ppermute | solution.py:45
  267.1 15.5 %collective-permute-start.25 = (bf16[4,288,192]{2,1,0:T(8,128)(2,1)S(1)}, bf16[4,288,192]{2,1,0:T(8,128)(2,1)S(1)}, u32[]{:S(2)}, u32[]{:S(2)}) collective-permute-start(bf16[4,288,192]{2,1,0:T(8,128)(2,1)S(1)} %fusion.58), channel_id=1, source_target_pairs={{0,4},{4,0},{8,12},{12,8},{16,20},{20,16},{24,28},{28,24},{1,5},{5... | collective-permute-start | bytes 1327112 | tf_op jit(solution)/shard_map/ppermute | solution.py:45
  267.7 16.9 %collective-permute-start.35 = (bf16[1,96,768]{2,1,0:T(8,128)(2,1)S(1)}, bf16[1,96,768]{2,1,0:T(8,128)(2,1)S(1)}, u32[]{:S(2)}, u32[]{:S(2)}) collective-permute-start(bf16[1,96,768]{2,1,0:T(8,128)(2,1)S(1)} %dynamic-slice_convert_fusion.5), channel_id=1, source_target_pairs={{0,16},{4,20},{8,24},{12,28},{16,0},{20,4},{24,8},{28,12},{1,17},{... | collective-permute-start | bytes 442376 | tf_op jit(solution)/shard_map/ppermute | solution.py:45
  269.3 23.6 %collective-permute-start.33 = (bf16[1,96,768]{2,1,0:T(8,128)(2,1)S(1)}, bf16[1,96,768]{2,1,0:T(8,128)(2,1)S(1)}, u32[]{:S(2)}, u32[]{:S(2)}) collective-permute-start(bf16[1,96,768]{2,1,0:T(8,128)(2,1)S(1)} %dynamic-slice_convert_fusion.6), channel_id=1, source_target_pairs={{0,16},{4,20},{8,24},{12,28},{16,0},{20,4},{24,8},{28,12},{1,17},{... | collective-permute-start | bytes 442376 | tf_op jit(solution)/shard_map/ppermute | solution.py:45
  282.8 8.3 %collective-permute-start.26 = (bf16[2,288,192]{2,1,0:T(8,128)(2,1)S(1)}, bf16[2,288,192]{2,1,0:T(8,128)(2,1)S(1)}, u32[]{:S(2)}, u32[]{:S(2)}) collective-permute-start(bf16[2,288,192]{2,1,0:T(8,128)(2,1)S(1)} %fusion.61), channel_id=1, source_target_pairs={{0,8},{4,12},{8,0},{12,4},{16,24},{20,28},{24,16},{28,20},{1,9},{5... | collective-permute-start | bytes 663560 | tf_op jit(solution)/shard_map/ppermute | solution.py:45
  292.7 8.6 %collective-permute-start.27 = (bf16[1,288,192]{2,1,0:T(8,128)(2,1)}, bf16[1,288,192]{2,1,0:T(8,128)(2,1)}, u32[]{:S(2)}, u32[]{:S(2)}) collective-permute-start(bf16[1,288,192]{2,1,0:T(8,128)(2,1)} %dynamic-slice_convert_fusion.8), channel_id=1, source_target_pairs={{0,16},{4,20},{8,24},{12,28},{16,0},{20,4},{24,8},{28,12},{1,17},{... | collective-permute-start | bytes 331784 | tf_op jit(solution)/shard_map/ppermute | solution.py:45
  (59 other events, 377.1 us)
